TPU v7x, 32 devices: a whole 2x2x4 slice. The times are simulated.
32 devices in a mesh: row: 8 (over z, y), col: 4 (over x, core).
Axes of the slice: x: 2, y: 2, z: 4, core: 2. Of those that a mesh axis runs over, the one named last changes fastest.
Arguments:
- inputs: bfloat16 [128, 8192], P('row', 'col'), may hold values from -6 to 6
- out_grad: bfloat16 [128, 8192], P('row', 'col'), may hold values from -96 to 96
- gate_weight: bfloat16 [8192, 16384], P('col', 'row'), may hold values from -0.0625 to 0.0625
- up_weight: bfloat16 [8192, 16384], P('col', 'row'), may hold values from -0.0625 to 0.0625
- down_weight: bfloat16 [16384, 8192], P('row', 'col'), may hold values from -0.046875 to 0.046875
Outputs:
- input_grad: bfloat16 [128, 8192], P('row', 'col')
- gate_grad: bfloat16 [8192, 16384], P('col', 'row')
- up_grad: bfloat16 [8192, 16384], P('col', 'row')
- down_grad: bfloat16 [16384, 8192], P('row', 'col')
All inputs are finite; a program needn't handle non-finite values.
Results may differ from a plain program's by a relative error of at most 0.005.
Values may be sent and summed in bfloat16 or wider, within the bound.
No kernel may reach another device: no remote copies, remote signals or barrier semaphores. Data moves between devices by JAX's collectives and lax.ppermute only.
A program may use at most 128 MiB of HBM per device.

v0:
```python
import jax
import jax.numpy as jnp
from jax import lax
from jax.sharding import PartitionSpec as P

LAYERS = 128


def contract_rows(left, right):
    return lax.dot_general(
        left, right, (((0,), (0,)), ((), ())), preferred_element_type=jnp.float32
    )


def contract_cols(left, right):
    return lax.dot_general(
        left, right, (((1,), (1,)), ((), ())), preferred_element_type=jnp.float32
    )


def gated_parts(gate, up, back, mult):
    sig = jax.nn.sigmoid(gate)
    hidden_grad = mult * back
    hidden = (gate * sig * up).astype(jnp.bfloat16)
    gate_delta = (hidden_grad * up * sig * (1.0 + gate * (1.0 - sig))).astype(jnp.bfloat16)
    up_delta = (hidden_grad * gate * sig).astype(jnp.bfloat16)
    return (hidden, gate_delta, up_delta)


def per_device(inputs, out_grad, gate_weight, up_weight, down_weight):
    mult = (2.0 * LAYERS) ** (-0.5)
    tokens_all = lax.all_gather(inputs, "row", axis=0, tiled=True)
    grads_all = lax.all_gather(out_grad, "row", axis=0, tiled=True)
    gate_part = jnp.dot(tokens_all, gate_weight, preferred_element_type=jnp.float32)
    up_part = jnp.dot(tokens_all, up_weight, preferred_element_type=jnp.float32)
    back_part = contract_cols(grads_all, down_weight)
    gate, up, back = lax.psum((gate_part, up_part, back_part), "col")
    hidden, gate_delta, up_delta = gated_parts(gate, up, back, mult)
    down_grad = (mult * contract_rows(hidden, grads_all)).astype(jnp.bfloat16)
    gate_grad = contract_rows(tokens_all, gate_delta).astype(jnp.bfloat16)
    up_grad = contract_rows(tokens_all, up_delta).astype(jnp.bfloat16)
    input_part = contract_cols(gate_delta, gate_weight) + contract_cols(up_delta, up_weight)
    input_grad = lax.psum_scatter(input_part, "row", scatter_dimension=0, tiled=True).astype(
        jnp.bfloat16
    )
    return (input_grad, gate_grad, up_grad, down_grad)


def solution(mesh):
    return jax.shard_map(
        per_device,
        mesh=mesh,
        in_specs=(
            P("row", "col"),
            P("row", "col"),
            P("col", "row"),
            P("col", "row"),
            P("row", "col"),
        ),
        out_specs=(P("row", "col"), P("col", "row"), P("col", "row"), P("row", "col")),
        check_vma=False,
    )
```

profile of v0, /device:TPU:0, one launch (start us, length us, event | category | flops | bytes accessed | tf_op | source)
XLA Modules:
  0.0 242.4 jit_solution(15786650038856876526)
XLA Ops:
  7.2 0.0 all-reduce.3.cloned.1.call-start
  7.2 0.0 slice-start
  7.2 33.4 %all_gather.7 = bf16[128,2048]{1,0:T(8,128)(2,1)S(1)} all-gather(bf16[16,2048]{1,0:T(8,128)(2,1)} %param.5), channel_id=1, replica_groups=mesh['row'=8,'col'=4] {'row'}, dimensions={0}, use_global_device_ids=true | all-gather | bytes 589824 | tf_op jit(solution)/shard_map/all_gather | solution.py:32
  40.6 5.8 %fusion.4 = f32[128,2048]{1,0:T(8,128)} fusion(bf16[128,2048]{1,0:T(8,128)(2,1)S(1)} %all_gather.7, bf16[2048,2048]{1,0:T(8,128)(2,1)} %param.7), kind=kOutput, calls=%fused_computation.12 | convolution fusion | flops 1073741824 | bytes 9961472 | tf_op jit(solution)/shard_map/dot_general | solution.py:34
  46.4 0.0 slice-done
  46.4 0.0 slice-start.3
  46.4 2.3 fusion.3
  48.7 31.3 %all_gather.6 = bf16[128,2048]{1,0:T(8,128)(2,1)S(1)} all-gather(bf16[16,2048]{1,0:T(8,128)(2,1)S(1)} %copy-done.2), channel_id=1, replica_groups=mesh['row'=8,'col'=4] {'row'}, dimensions={0}, use_global_device_ids=true | all-gather | bytes 589824 | tf_op jit(solution)/shard_map/all_gather | solution.py:33
  79.9 3.9 %fusion.2 = f32[128,2048]{1,0:T(8,128)} fusion(bf16[128,2048]{1,0:T(8,128)(2,1)S(1)} %all_gather.6, bf16[2048,2048]{1,0:T(8,128)(2,1)S(1)} %bitcast.22), kind=kOutput, calls=%fused_computation.10 | convolution fusion | flops 1073741824 | bytes 9961472 | tf_op jit(solution)/shard_map/dot_general | solution.py:16
  83.8 0.0 all-reduce.3.cloned.1.call-update
  83.8 0.2 reduce-scatter.2.cloned.1.call-start
  84.1 69.6 %all-reduce.3.cloned.1.call-done = (f32[128,2048]{1,0:T(8,128)}, f32[128,2048]{1,0:T(8,128)}, f32[128,2048]{1,0:T(8,128)}) async-done(((f32[128,2048]{1,0:T(8,128)}, f32[128,2048]{1,0:T(8,128)}, f32[128,2048]{1,0:T(8,128)}), (f32[128,2048]{1,0:T(8,128)}, f32[128,2048]{1,0:T(8,128)}, f32[128,2048]{1,0:T(8,128)})) %all-reduce.3.cloned.1.call-update) | async-done | bytes 3145744 | tf_op jit(solution)/shard_map/psum | solution.py:37
  153.7 2.3 multiply_convert_fusion.2
  156.0 6.3 %fusion.5 = f32[128,2048]{1,0:T(8,128)S(1)} fusion(bf16[128,2048]{1,0:T(8,128)(2,1)S(1)} %get-tuple-element.12, bf16[2048,2048]{1,0:T(8,128)(2,1)} %param.7), kind=kOutput, calls=%fused_computation.13 | convolution fusion | flops 1073741824 | bytes 9961472 | tf_op jit(solution)/shard_map/dot_general | solution.py:16
  162.3 7.3 %convolution_add_fusion = f32[128,2048]{1,0:T(8,128)} fusion(f32[128,2048]{1,0:T(8,128)S(1)} %fusion.5, bf16[128,2048]{1,0:T(8,128)(2,1)S(1)} %get-tuple-element.11, bf16[2048,2048]{1,0:T(8,128)(2,1)} %param.8), kind=kOutput, calls=%fused_computation.3 | convolution fusion | flops 1074003968 | bytes 11010048 | tf_op jit(solution)/shard_map/dot_general | solution.py:16
  169.5 0.0 reduce-scatter.2.cloned.1.call-update
  169.6 5.8 %convert_bitcast_fusion.1 = bf16[2048,2048]{0,1:T(8,128)(2,1)} fusion(bf16[128,2048]{1,0:T(8,128)(2,1)S(1)} %get-tuple-element.12, bf16[128,2048]{1,0:T(8,128)(2,1)S(1)} %all_gather.7), kind=kOutput, calls=%fused_computation.2 | convolution fusion | flops 1077936128 | bytes 9437184 | tf_op jit(solution)/shard_map/dot_general | solution.py:10
  175.3 12.2 %copy.9 = bf16[2048,2048]{1,0:T(8,128)(2,1)} copy(bf16[2048,2048]{0,1:T(8,128)(2,1)} %convert_bitcast_fusion.1) | data formatting | bytes 16777216
  187.6 5.8 %convert_bitcast_fusion = bf16[2048,2048]{0,1:T(8,128)(2,1)} fusion(bf16[128,2048]{1,0:T(8,128)(2,1)S(1)} %get-tuple-element.11, bf16[128,2048]{1,0:T(8,128)(2,1)S(1)} %all_gather.7), kind=kOutput, calls=%fused_computation.1 | convolution fusion | flops 1077936128 | bytes 9437184 | tf_op jit(solution)/shard_map/dot_general | solution.py:10
  193.3 12.4 %copy.10 = bf16[2048,2048]{1,0:T(8,128)(2,1)} copy(bf16[2048,2048]{0,1:T(8,128)(2,1)} %convert_bitcast_fusion) | data formatting | bytes 16777216
  205.7 0.0 copy-done
  205.7 5.8 %multiply_convert_fusion = bf16[2048,2048]{1,0:T(8,128)(2,1)} fusion(bf16[128,2048]{1,0:T(8,128)(2,1)S(1)} %all_gather.6, f32[128,2048]{1,0:T(8,128)S(1)} %copy-done.1, f32[128,2048]{1,0:T(8,128)S(1)} %copy-done), kind=kOutput, calls=%fused_computation | convolution fusion | flops 1083703296 | bytes 11010048 | tf_op jit(solution)/shard_map/dot_general | solution.py:10
  211.5 22.4 %reduce-scatter.2.cloned.1.call-done = f32[16,2048]{1,0:T(8,128)} async-done(((f32[128,2048]{1,0:T(8,128)}), f32[16,2048]{1,0:T(8,128)}) %reduce-scatter.2.cloned.1.call-update) | async-done | bytes 131088 | tf_op jit(solution)/shard_map/reduce_scatter | solution.py:43
  234.0 1.5 convert_element_type.29
  (12 shorter events, 0.0 us)
Async XLA Ops:
  7.2 146.5 %all-reduce.3.cloned.1.call-start = ((), (), s32[]{:S(2)}) async-start(), calls=%async_computation.2 | async-start | bytes 6291456 | tf_op jit(solution)/shard_map/psum | solution.py:37
  7.2 39.2 %slice-start = ((s8[8388608]{0:T(1024)(128)(4,1)}), s8[4194304]{0:T(1024)(128)(4,1)S(1)}, s32[]{:S(2)}) async-start(s8[8388608]{0:T(1024)(128)(4,1)} %bitcast.19), calls=%async_computation.3 | async-start | bytes 8388608
  40.6 5.8 %slice-start.1 = ((s8[8388608]{0:T(1024)(128)(4,1)}), s8[4194304]{0:T(1024)(128)(4,1)S(1)}, s32[]{:S(2)}) async-start(s8[8388608]{0:T(1024)(128)(4,1)} %bitcast.19), calls=%async_computation.4 | async-start | bytes 8388608
  40.6 39.3 %slice-start.2 = ((s8[8388608]{0:T(1024)(128)(4,1)}), s8[4194304]{0:T(1024)(128)(4,1)S(1)}, s32[]{:S(2)}) async-start(s8[8388608]{0:T(1024)(128)(4,1)} %bitcast.21), calls=%async_computation.5 | async-start | bytes 8388608
  46.4 2.3 copy-start.2
  46.4 33.6 %slice-start.3 = ((s8[8388608]{0:T(1024)(128)(4,1)}), s8[4194304]{0:T(1024)(128)(4,1)S(1)}, s32[]{:S(2)}) async-start(s8[8388608]{0:T(1024)(128)(4,1)} %bitcast.21), calls=%async_computation.6 | async-start | bytes 8388608
  83.8 150.2 %reduce-scatter.2.cloned.1.call-start = ((), (), s32[]{:S(2)}) async-start(), calls=%async_computation.1 | async-start | bytes 1179648 | tf_op jit(solution)/shard_map/reduce_scatter | solution.py:43
  193.3 12.4 %copy-start = (f32[128,2048]{1,0:T(8,128)S(1)}, f32[128,2048]{1,0:T(8,128)}, u32[]{:S(2)}) copy-start(f32[128,2048]{1,0:T(8,128)} %get-tuple-element.8) | copy-start | bytes 3145732
  193.3 12.4 %copy-start.1 = (f32[128,2048]{1,0:T(8,128)S(1)}, f32[128,2048]{1,0:T(8,128)}, u32[]{:S(2)}) copy-start(f32[128,2048]{1,0:T(8,128)} %get-tuple-element.9) | copy-start | bytes 3145732
Sparse Core Ops, SparseCore 0:
  83.9 69.6 all-reduce.2
  169.7 64.2 reduce-scatter.1
where the time goes:
time: 243 us; the launch traced here: 242 us
  waiting for transfers between devices  92.1 us (38%)
  blocking collectives  64.6 us (27%)
  matrix products  42.8 us (18%)
  local copies, waits for them, and re-layouts  24.7 us (10%)
  between operations  14.1 us (6%)
  other arithmetic  3.89 us (2%)
    psum x1, waiting for transfers between devices, per_device(): gate, up, back = lax.psum((gate_part, up_part, back_part), 'col')  69.6 us
    all_gather x1, blocking collectives, per_device(): tokens_all = lax.all_gather(inputs, 'row', axis=0, tiled=True)  33.4 us
    all_gather x1, blocking collectives, per_device(): grads_all = lax.all_gather(out_grad, 'row', axis=0, tiled=True)  31.3 us
    unnamed x16, local copies, waits for them, and re-layouts  24.7 us
    reduce_scatter x1, waiting for transfers between devices, per_device(): lax.psum_scatter(input_part, 'row', scatter_dimension=0, tiled=True)  22.4 us
    dot_general x3, matrix products, contract_cols(): lax.dot_general(left, right, (((1,), (1,)), ((), ())), preferred_element_...  17.4 us
    dot_general x3, matrix products, contract_rows(): lax.dot_general(left, right, (((0,), (0,)), ((), ())), preferred_element_...  17.3 us
    dot_general x1, matrix products, per_device(): jnp.dot(tokens_all, gate_weight, preferred_element_type=jnp.float32)  5.76 us
  transfers between devices with their start and end apart: 2, of which 2 were waited for; matrix products, arithmetic and copies ran while one was open for 17% of the time, Pallas kernels for 0%

commit v1 on v0

--- a/solution.py
+++ b/solution.py
@@ -1,9 +1,28 @@
+import functools
 import jax
 import jax.numpy as jnp
 from jax import lax
 from jax.sharding import PartitionSpec as P
 
 LAYERS = 128
+
+
+def edit_the_rounds(tile_in, peer_axis):
+    n_slots = lax.axis_size(peer_axis)
+    history = []
+    for rr in range(n_slots):
+        history.append((rr, (rr + 1) % n_slots))
+
+    def map_sources_all(y2):
+        if len(y2) == n_slots:
+            return y2
+        return map_sources_all([lax.ppermute(y2[0], peer_axis, history), *y2])
+
+    formed = jnp.concatenate(map_sources_all([tile_in]), axis=0)
+    return jnp.roll(formed, (lax.axis_index(peer_axis) + 1) * tile_in.shape[0], axis=0)
+
+
+part_the_threads = functools.partial(edit_the_rounds, peer_axis="row")
 
 
 def contract_rows(left, right):
@@ -29,7 +48,7 @@
 
 def per_device(inputs, out_grad, gate_weight, up_weight, down_weight):
     mult = (2.0 * LAYERS) ** (-0.5)
-    tokens_all = lax.all_gather(inputs, "row", axis=0, tiled=True)
+    tokens_all = part_the_threads(inputs)
     grads_all = lax.all_gather(out_grad, "row", axis=0, tiled=True)
     gate_part = jnp.dot(tokens_all, gate_weight, preferred_element_type=jnp.float32)
     up_part = jnp.dot(tokens_all, up_weight, preferred_element_type=jnp.float32)

time: 243 us -> 251 us (1.033)
  waiting for transfers between devices: 92.1 us -> 149 us
  blocking collectives: 64.6 us -> 31.7 us
  local copies, waits for them, and re-layouts: 24.7 us -> 0.13 us
  starting transfers between devices: 0.26 us -> 5.24 us
  matrix products: 42.8 us -> 46.1 us
    ppermute x0 -> x7, waiting for transfers between devices: none -> 33.7 us  [map_sources_all(): return map_sources_all([lax.ppermute(y2[0], peer_axis, history), *y2])]
    all_gather x1 -> x0, blocking collectives: 33.4 us -> none  [per_device(): tokens_all = lax.all_gather(inputs, 'row', axis=0, tiled=True)]
    reduce_scatter x1, waiting for transfers between devices: 22.4 us -> 47 us  [per_device(): lax.psum_scatter(input_part, 'row', scatter_dimension=0, tiled=True)]
    unnamed x16 -> x25, local copies, waits for them, and re-layouts: 24.7 us -> 0.13 us
    ppermute x0 -> x7, starting transfers between devices: none -> 4.98 us  [map_sources_all(): return map_sources_all([lax.ppermute(y2[0], peer_axis, history), *y2])]
    dot_general x3, matrix products: 17.4 us -> 20.7 us  [contract_cols(): lax.dot_general(left, right, (((1,), (1,)), ((), ())), preferred_element_...]
  transfers between devices with their start and end apart: 2 -> 9, of which waited for: 2 -> 7; matrix products, arithmetic and copies ran while one was open for 17% -> 10% of each run, Pallas kernels for 0% -> 0%
where the time goes in v1:
time: 251 us
  waiting for transfers between devices  149 us (59%)
  matrix products  46.1 us (18%)
  blocking collectives  31.7 us (13%)
  between operations  14.2 us (6%)
  starting transfers between devices  5.24 us (2%)
  other arithmetic  3.88 us (2%)
    psum x1, waiting for transfers between devices, per_device(): gate, up, back = lax.psum((gate_part, up_part, back_part), 'col')  68.6 us
    reduce_scatter x1, waiting for transfers between devices, per_device(): lax.psum_scatter(input_part, 'row', scatter_dimension=0, tiled=True)  47 us
    ppermute x7, waiting for transfers between devices, map_sources_all(): return map_sources_all([lax.ppermute(y2[0], peer_axis, history), *y2])  33.7 us
    all_gather x1, blocking collectives, per_device(): grads_all = lax.all_gather(out_grad, 'row', axis=0, tiled=True)  31.7 us
    dot_general x3, matrix products, contract_cols(): lax.dot_general(left, right, (((1,), (1,)), ((), ())), preferred_element_...  20.7 us
    dot_general x3, matrix products, contract_rows(): lax.dot_general(left, right, (((0,), (0,)), ((), ())), preferred_element_...  17.4 us
    dot_general x1, matrix products, per_device(): jnp.dot(tokens_all, gate_weight, preferred_element_type=jnp.float32)  5.76 us
  transfers between devices with their start and end apart: 9, of which 7 were waited for; matrix products, arithmetic and copies ran while one was open for 10% of the time, Pallas kernels for 0%

profile of v1, /device:TPU:0, one launch (start us, length us, event | category | flops | bytes accessed | tf_op | source)
XLA Modules:
  0.0 250.6 jit_solution(9769457856488640433)
XLA Ops:
  7.2 0.0 all-reduce.3.cloned.1.call-start
  7.2 3.0 %collective-permute-start = (bf16[16,2048]{1,0:T(8,128)(2,1)}, bf16[16,2048]{1,0:T(8,128)(2,1)S(1)}, u32[]{:S(2)}, u32[]{:S(2)}) collective-permute-start(bf16[16,2048]{1,0:T(8,128)(2,1)} %param.5), channel_id=1, source_target_pairs={{0,4},{4,8},{8,12},{12,16},{16,20},{20,24},{24,28},{28,0},{1,5},{5... | collective-permute-start | bytes 196616 | tf_op jit(solution)/shard_map/ppermute | solution.py:19
  10.3 5.5 %collective-permute-done = bf16[16,2048]{1,0:T(8,128)(2,1)S(1)} collective-permute-done((bf16[16,2048]{1,0:T(8,128)(2,1)}, bf16[16,2048]{1,0:T(8,128)(2,1)S(1)}, u32[]{:S(2)}, u32[]{:S(2)}) %collective-permute-start) | collective-permute-done | bytes 65568 | tf_op jit(solution)/shard_map/ppermute | solution.py:19
  15.8 7.0 %collective-permute-done.1 = bf16[16,2048]{1,0:T(8,128)(2,1)S(1)} collective-permute-done((bf16[16,2048]{1,0:T(8,128)(2,1)S(1)}, bf16[16,2048]{1,0:T(8,128)(2,1)S(1)}, u32[]{:S(2)}, u32[]{:S(2)}) %collective-permute-start.1) | collective-permute-done | bytes 65568 | tf_op jit(solution)/shard_map/ppermute | solution.py:19
  22.7 7.0 %collective-permute-done.2 = bf16[16,2048]{1,0:T(8,128)(2,1)S(1)} collective-permute-done((bf16[16,2048]{1,0:T(8,128)(2,1)S(1)}, bf16[16,2048]{1,0:T(8,128)(2,1)S(1)}, u32[]{:S(2)}, u32[]{:S(2)}) %collective-permute-start.2) | collective-permute-done | bytes 65568 | tf_op jit(solution)/shard_map/ppermute | solution.py:19
  29.7 7.0 %collective-permute-done.3 = bf16[16,2048]{1,0:T(8,128)(2,1)S(1)} collective-permute-done((bf16[16,2048]{1,0:T(8,128)(2,1)S(1)}, bf16[16,2048]{1,0:T(8,128)(2,1)S(1)}, u32[]{:S(2)}, u32[]{:S(2)}) %collective-permute-start.3) | collective-permute-done | bytes 65568 | tf_op jit(solution)/shard_map/ppermute | solution.py:19
  36.7 7.3 %collective-permute-done.4 = bf16[16,2048]{1,0:T(8,128)(2,1)S(1)} collective-permute-done((bf16[16,2048]{1,0:T(8,128)(2,1)S(1)}, bf16[16,2048]{1,0:T(8,128)(2,1)S(1)}, u32[]{:S(2)}, u32[]{:S(2)}) %collective-permute-start.4) | collective-permute-done | bytes 65568 | tf_op jit(solution)/shard_map/ppermute | solution.py:19
  44.0 31.7 %all_gather.3 = bf16[128,2048]{1,0:T(8,128)(2,1)S(1)} all-gather(bf16[16,2048]{1,0:T(8,128)(2,1)} %param.6), channel_id=1, replica_groups=mesh['row'=8,'col'=4] {'row'}, dimensions={0}, use_global_device_ids=true | all-gather | bytes 589824 | tf_op jit(solution)/shard_map/all_gather | solution.py:52
  75.6 1.9 collective-permute-start.6
  77.6 7.2 %fusion.12 = f32[128,2048]{1,0:T(8,128)} fusion(bf16[128,2048]{1,0:T(8,128)(2,1)S(1)} %all_gather.3, bf16[2048,2048]{1,0:T(8,128)(2,1)} %param.9), kind=kOutput, calls=%fused_computation.36 | convolution fusion | flops 1073741824 | bytes 9961472 | tf_op jit(solution)/shard_map/dot_general | solution.py:35
  85.1 5.8 %fusion.3 = f32[128,2048]{1,0:T(8,128)} fusion(bf16[2048,2048]{1,0:T(8,128)(2,1)} %param.7, bf16[256,2048]{1,0:T(8,128)(2,1)S(1)} %constant_dynamic-update-slice_fusion, s32[]{:T(128)S(6)} %select_n.14), kind=kOutput, calls=%fused_computation.11 | convolution fusion | flops 1073741824 | bytes 9961476 | tf_op jit(solution)/shard_map/dot_general | solution.py:53
  90.8 2.3 fusion.5
  93.1 0.0 all-reduce.3.cloned.1.call-update
  93.1 0.2 reduce-scatter.2.cloned.1.call-start
  93.4 68.6 %all-reduce.3.cloned.1.call-done = (f32[128,2048]{1,0:T(8,128)}, f32[128,2048]{1,0:T(8,128)}, f32[128,2048]{1,0:T(8,128)}) async-done(((f32[128,2048]{1,0:T(8,128)}, f32[128,2048]{1,0:T(8,128)}, f32[128,2048]{1,0:T(8,128)}), (f32[128,2048]{1,0:T(8,128)}, f32[128,2048]{1,0:T(8,128)}, f32[128,2048]{1,0:T(8,128)})) %all-reduce.3.cloned.1.call-update) | async-done | bytes 3145744 | tf_op jit(solution)/shard_map/psum | solution.py:56
  162.0 2.3 multiply_convert_fusion.2
  164.3 6.3 %fusion.13 = f32[128,2048]{1,0:T(8,128)S(1)} fusion(bf16[128,2048]{1,0:T(8,128)(2,1)S(1)} %get-tuple-element.8, bf16[2048,2048]{1,0:T(8,128)(2,1)} %param.7), kind=kOutput, calls=%fused_computation.37 | convolution fusion | flops 1073741824 | bytes 9961472 | tf_op jit(solution)/shard_map/dot_general | solution.py:35
  170.6 7.3 %convolution_add_fusion = f32[128,2048]{1,0:T(8,128)} fusion(f32[128,2048]{1,0:T(8,128)S(1)} %fusion.13, bf16[128,2048]{1,0:T(8,128)(2,1)S(1)} %get-tuple-element.7, bf16[2048,2048]{1,0:T(8,128)(2,1)} %param.8), kind=kOutput, calls=%fused_computation.3 | convolution fusion | flops 1074003968 | bytes 11010048 | tf_op jit(solution)/shard_map/dot_general | solution.py:35
  177.8 0.0 reduce-scatter.2.cloned.1.call-update
  177.9 5.8 %convolution_convert_fusion = bf16[2048,2048]{1,0:T(8,128)(2,1)} fusion(bf16[128,2048]{1,0:T(8,128)(2,1)S(1)} %get-tuple-element.7, bf16[256,2048]{1,0:T(8,128)(2,1)S(1)} %constant_dynamic-update-slice_fusion, s32[]{:T(128)S(6)} %select_n.14), kind=kOutput, calls=%fused_computation.1 | convolution fusion | flops 1077936128 | bytes 9437188 | tf_op jit(solution)/shard_map/dot_general | solution.py:29
  183.6 5.8 %convolution_convert_fusion.1 = bf16[2048,2048]{1,0:T(8,128)(2,1)} fusion(bf16[128,2048]{1,0:T(8,128)(2,1)S(1)} %get-tuple-element.8, bf16[256,2048]{1,0:T(8,128)(2,1)S(1)} %constant_dynamic-update-slice_fusion, s32[]{:T(128)S(6)} %select_n.14), kind=kOutput, calls=%fused_computation.2 | convolution fusion | flops 1077936128 | bytes 9437188 | tf_op jit(solution)/shard_map/dot_general | solution.py:29
  189.4 5.8 %multiply_convert_fusion = bf16[2048,2048]{1,0:T(8,128)(2,1)} fusion(bf16[128,2048]{1,0:T(8,128)(2,1)S(1)} %all_gather.3, f32[128,2048]{1,0:T(8,128)S(1)} %copy-done.1, f32[128,2048]{1,0:T(8,128)S(1)} %copy-done), kind=kOutput, calls=%fused_computation | convolution fusion | flops 1083703296 | bytes 11010048 | tf_op jit(solution)/shard_map/dot_general | solution.py:29
  195.2 47.0 %reduce-scatter.2.cloned.1.call-done = f32[16,2048]{1,0:T(8,128)} async-done(((f32[128,2048]{1,0:T(8,128)}), f32[16,2048]{1,0:T(8,128)}) %reduce-scatter.2.cloned.1.call-update) | async-done | bytes 131088 | tf_op jit(solution)/shard_map/reduce_scatter | solution.py:62
  242.3 1.5 convert_element_type.23
  (34 shorter events, 0.2 us)
Async XLA Ops:
  7.2 77.7 %copy-start.2 = (bf16[16,2048]{1,0:T(8,128)(2,1)S(1)}, bf16[16,2048]{1,0:T(8,128)(2,1)}, u32[]{:S(2)}) copy-start(bf16[16,2048]{1,0:T(8,128)(2,1)} %param.5) | copy-start | bytes 196612
  7.2 154.8 %all-reduce.3.cloned.1.call-start = ((), (), s32[]{:S(2)}) async-start(), calls=%async_computation.2 | async-start | bytes 6291456 | tf_op jit(solution)/shard_map/psum | solution.py:56
  7.2 8.5 %collective-permute-start = (bf16[16,2048]{1,0:T(8,128)(2,1)}, bf16[16,2048]{1,0:T(8,128)(2,1)S(1)}, u32[]{:S(2)}, u32[]{:S(2)}) collective-permute-start(bf16[16,2048]{1,0:T(8,128)(2,1)} %param.5), channel_id=1, source_target_pairs={{0,4},{4,8},{8,12},{12,16},{16,20},{20,24},{24,28},{28,0},{1,5},{5... | collective-permute-start | bytes 196616 | tf_op jit(solution)/shard_map/ppermute | solution.py:19
  15.8 7.0 %collective-permute-start.1 = (bf16[16,2048]{1,0:T(8,128)(2,1)S(1)}, bf16[16,2048]{1,0:T(8,128)(2,1)S(1)}, u32[]{:S(2)}, u32[]{:S(2)}) collective-permute-start(bf16[16,2048]{1,0:T(8,128)(2,1)S(1)} %collective-permute-done), channel_id=1, source_target_pairs={{0,4},{4,8},{8,12},{12,16},{16,20},{20,24},{24,28},{28,0},{1,5},{5... | collective-permute-start | bytes 196616 | tf_op jit(solution)/shard_map/ppermute | solution.py:19
  22.7 7.0 %collective-permute-start.2 = (bf16[16,2048]{1,0:T(8,128)(2,1)S(1)}, bf16[16,2048]{1,0:T(8,128)(2,1)S(1)}, u32[]{:S(2)}, u32[]{:S(2)}) collective-permute-start(bf16[16,2048]{1,0:T(8,128)(2,1)S(1)} %collective-permute-done.1), channel_id=1, source_target_pairs={{0,4},{4,8},{8,12},{12,16},{16,20},{20,24},{24,28},{28,0},{1,5},{5... | collective-permute-start | bytes 196616 | tf_op jit(solution)/shard_map/ppermute | solution.py:19
  29.7 7.0 %collective-permute-start.3 = (bf16[16,2048]{1,0:T(8,128)(2,1)S(1)}, bf16[16,2048]{1,0:T(8,128)(2,1)S(1)}, u32[]{:S(2)}, u32[]{:S(2)}) collective-permute-start(bf16[16,2048]{1,0:T(8,128)(2,1)S(1)} %collective-permute-done.2), channel_id=1, source_target_pairs={{0,4},{4,8},{8,12},{12,16},{16,20},{20,24},{24,28},{28,0},{1,5},{5... | collective-permute-start | bytes 196616 | tf_op jit(solution)/shard_map/ppermute | solution.py:19
  36.7 7.3 %collective-permute-start.4 = (bf16[16,2048]{1,0:T(8,128)(2,1)S(1)}, bf16[16,2048]{1,0:T(8,128)(2,1)S(1)}, u32[]{:S(2)}, u32[]{:S(2)}) collective-permute-start(bf16[16,2048]{1,0:T(8,128)(2,1)S(1)} %collective-permute-done.3), channel_id=1, source_target_pairs={{0,4},{4,8},{8,12},{12,16},{16,20},{20,24},{24,28},{28,0},{1,5},{5... | collective-permute-start | bytes 196616 | tf_op jit(solution)/shard_map/ppermute | solution.py:19
  44.0 31.7 %collective-permute-start.5 = (bf16[16,2048]{1,0:T(8,128)(2,1)S(1)}, bf16[16,2048]{1,0:T(8,128)(2,1)S(1)}, u32[]{:S(2)}, u32[]{:S(2)}) collective-permute-start(bf16[16,2048]{1,0:T(8,128)(2,1)S(1)} %collective-permute-done.4), channel_id=1, source_target_pairs={{0,4},{4,8},{8,12},{12,16},{16,20},{20,24},{24,28},{28,0},{1,5},{5... | collective-permute-start | bytes 196616 | tf_op jit(solution)/shard_map/ppermute | solution.py:19
  75.6 9.1 %collective-permute-start.6 = (bf16[16,2048]{1,0:T(8,128)(2,1)S(1)}, bf16[16,2048]{1,0:T(8,128)(2,1)S(1)}, u32[]{:S(2)}, u32[]{:S(2)}) collective-permute-start(bf16[16,2048]{1,0:T(8,128)(2,1)S(1)} %collective-permute-done.5), channel_id=1, source_target_pairs={{0,4},{4,8},{8,12},{12,16},{16,20},{20,24},{24,28},{28,0},{1,5},{5... | collective-permute-start | bytes 196616 | tf_op jit(solution)/shard_map/ppermute | solution.py:19
  84.8 6.0 %slice-start = ((s8[8388608]{0:T(1024)(128)(4,1)}), s8[4194304]{0:T(1024)(128)(4,1)S(1)}, s32[]{:S(2)}) async-start(s8[8388608]{0:T(1024)(128)(4,1)} %bitcast.11), calls=%async_computation.3 | async-start | bytes 8388608
  85.0 5.8 %slice-start.1 = ((s8[8388608]{0:T(1024)(128)(4,1)}), s8[4194304]{0:T(1024)(128)(4,1)S(1)}, s32[]{:S(2)}) async-start(s8[8388608]{0:T(1024)(128)(4,1)} %bitcast.11), calls=%async_computation.4 | async-start | bytes 8388608
  93.1 149.1 %reduce-scatter.2.cloned.1.call-start = ((), (), s32[]{:S(2)}) async-start(), calls=%async_computation.1 | async-start | bytes 1179648 | tf_op jit(solution)/shard_map/reduce_scatter | solution.py:62
  183.6 5.8 %copy-start = (f32[128,2048]{1,0:T(8,128)S(1)}, f32[128,2048]{1,0:T(8,128)}, u32[]{:S(2)}) copy-start(f32[128,2048]{1,0:T(8,128)} %get-tuple-element.4) | copy-start | bytes 3145732
  183.6 5.8 %copy-start.1 = (f32[128,2048]{1,0:T(8,128)S(1)}, f32[128,2048]{1,0:T(8,128)}, u32[]{:S(2)}) copy-start(f32[128,2048]{1,0:T(8,128)} %get-tuple-element.5) | copy-start | bytes 3145732
Sparse Core Ops, SparseCore 0:
  93.2 68.6 all-reduce.2
  178.0 64.2 reduce-scatter.1
